TPU v7x, 256 devices: a whole 4x4x8 slice. The times are simulated.
256 devices in a mesh: row: 16 (over y, z_lo), col: 16 (over z_hi, x, core).
Axes of the slice: x: 4, y: 4, z: 8 (z_hi: 2, z_lo: 4; z = z_hi * 4 + z_lo), core: 2. Of those that a mesh axis runs over, the one named last changes fastest.
Arguments:
- laplacian: float32 [23040, 23040], P('row', 'col'), may hold values from -1 to 1.12, as said below
- block: float32 [23040, 256], P(('row', 'col')), may hold values from -6 to 6
- bounds: float32 [2], replicated, may hold values from 0.25 to 2.1, as said below
Outputs:
- filtered: float32 [23040, 256], P(('row', 'col'))
- rayleigh: float32 [256, 256], replicated
Inputs may be any that keep to these rules, and one draw needn't show every extreme that they name: laplacian is symmetric; its diagonal entries lie in 0.88 to 1.12 and its other entries have magnitude at most 1.14 / sqrt(23040). bounds[0] lies in 0.25 to 0.40 and bounds[1] in 1.95 to 2.10.
All inputs are finite; a program needn't handle non-finite values.
Results may differ from a plain program's by a relative error of at most 0.00025.
Values sent between devices are 32-bit elements; how exact they have to be, the bound alone decides.
A program may use at most 64 MiB of HBM per device.

v0:
```python
import jax
import jax.numpy as jnp
from jax import lax
from jax.sharding import PartitionSpec as P


def relayout(panel_rows, row_index, col_index, tile_rows, tile_cols):
    offset = col_index * tile_cols - row_index * tile_rows
    zeros_pad = jnp.zeros((tile_cols, panel_rows.shape[1]), jnp.float32)
    padded = jnp.concatenate([zeros_pad, panel_rows, zeros_pad], axis=0)
    start_row = jnp.clip(offset + tile_cols, 0, tile_rows + tile_cols)
    sliced = lax.dynamic_slice_in_dim(padded, start_row, tile_cols, 0)
    target = offset + lax.broadcasted_iota(jnp.int32, (tile_cols, 1), 0)
    inside = (target >= 0) & (target < tile_rows)
    return jnp.where(inside, sliced, 0.0)


def body(laplacian, block, bounds):
    row_index = lax.axis_index("row")
    col_index = lax.axis_index("col")
    tile_rows, tile_cols = laplacian.shape
    lower_bound = bounds[0]
    upper_bound = bounds[1]
    center = (upper_bound + lower_bound) * 0.5
    half_width = (upper_bound - lower_bound) * 0.5
    factor_two = 2.0 / half_width
    global_rows = row_index * tile_rows + lax.broadcasted_iota(jnp.int32, (tile_rows, tile_cols), 0)
    global_cols = col_index * tile_cols + lax.broadcasted_iota(jnp.int32, (tile_rows, tile_cols), 1)
    shifted = laplacian - center * (global_rows == global_cols).astype(jnp.float32)

    def through_columns(panel_rows):
        return lax.dot_general(
            shifted,
            panel_rows,
            (((0,), (0,)), ((), ())),
            precision=lax.Precision.HIGHEST,
            preferred_element_type=jnp.float32,
        )

    def through_rows(panel_cols):
        return jnp.dot(
            shifted, panel_cols, precision=lax.Precision.HIGHEST, preferred_element_type=jnp.float32
        )

    def gather_rows(values):
        return lax.all_gather(values, "col", axis=0, tiled=True)

    def gather_cols(values):
        return lax.all_gather(values, "row", axis=0, tiled=True)

    def column_sum(values):
        return lax.psum_scatter(values, "row", scatter_dimension=0, tiled=True)

    def row_sum(values):
        return lax.psum_scatter(values, "col", scatter_dimension=0, tiled=True)

    filter_one = column_sum(through_columns(gather_rows(block))) / half_width
    filter_two = factor_two * row_sum(through_rows(gather_cols(filter_one))) - block
    filter_three = factor_two * column_sum(through_columns(gather_rows(filter_two))) - filter_one
    filter_four = factor_two * row_sum(through_rows(gather_cols(filter_three))) - filter_two
    panel_four = gather_rows(filter_four)
    dims_inner = (((0,), (0,)), ((), ()))
    image_piece, moved_piece = (
        lax.psum_scatter(through_columns(panel_four), "row", scatter_dimension=0, tiled=True),
        lax.psum_scatter(
            relayout(panel_four, row_index, col_index, tile_rows, tile_cols),
            "row",
            scatter_dimension=0,
            tiled=True,
        ),
    )
    gram_part = lax.dot_general(
        moved_piece,
        moved_piece,
        dims_inner,
        precision=lax.Precision.HIGHEST,
        preferred_element_type=jnp.float32,
    )
    image_part = lax.dot_general(
        moved_piece,
        image_piece,
        dims_inner,
        precision=lax.Precision.HIGHEST,
        preferred_element_type=jnp.float32,
    )
    gram, projected = lax.psum((gram_part, image_part), ("row", "col"))
    projected = projected + center * gram
    projected = (projected + projected.T) * 0.5
    factor = jnp.linalg.cholesky(gram)
    first_solve = jax.scipy.linalg.solve_triangular(factor, projected, lower=True)
    rayleigh = jax.scipy.linalg.solve_triangular(factor, first_solve.T, lower=True)
    return (filter_four, rayleigh)


def solution(mesh):
    placed = (P("row", "col"), P(("row", "col"), None), P())
    return jax.shard_map(
        body, mesh=mesh, in_specs=placed, out_specs=(P(("row", "col"), None), P()), check_vma=False
    )
```

profile of v0, /device:TPU:2, one launch (start us, length us, event | category | flops | bytes accessed | tf_op | source)
XLA Modules:
  0.0 1090.3 jit_solution(2360731310481953332)
XLA Ops:
  7.2 0.7 all-gather.11.cloned.1.call-update
  8.0 1.3 fusion.44
  10.6 61.9 %all-gather.11.cloned.1.call-done = f32[16,90,256]{2,1,0:T(8,128)} async-done(((f32[1,90,256]{2,1,0:T(8,128)}), f32[16,90,256]{2,1,0:T(8,128)}) %all-gather.11.cloned.1.call-update) | async-done | bytes 1474576 | tf_op jit(solution)/shard_map/all_gather | solution.py:46
  72.5 1.5 reshape.61
  74.0 17.9 %fusion.41 = f32[1440,256]{1,0:T(8,128)S(1)} fusion(f32[1440,256]{1,0:T(8,128)S(1)} %reshape.61, f32[1440,1440]{1,0:T(8,128)} %param.5, f32[]{:T(128)} %bitcast.1, s32[1440]{0:T(1024)S(1)} %get-tuple-element.45, s32[1440]{0:T(1024)S(1)} %get-tuple-element.46), kind=kOutput, calls=%fused_computation.71 | convolution fusion | flops 6376320000 | bytes 11255044 | tf_op jit(solution)/shard_map/dot_general | solution.py:32
  91.8 55.3 %fusion = f32[96,256]{1,0:T(8,128)S(1)} fusion(f32[1440,256]{1,0:T(8,128)S(1)} %fusion.41), kind=kCustom, calls=%all-reduce-scatter | all-reduce-scatter fusion | flops 393217 | bytes 1573888
  147.1 1.3 collective-permute-start
  152.2 80.0 %all-gather.13.cloned.1.call-done = f32[16,90,256]{2,1,0:T(8,128)} async-done(((f32[1,90,256]{2,1,0:T(8,128)}), f32[16,90,256]{2,1,0:T(8,128)}) %all-gather.13.cloned.1.call-update) | async-done | bytes 1474576 | tf_op jit(solution)/shard_map/all_gather | solution.py:49
  232.3 1.5 reshape.63
  233.8 10.1 fusion.40
  243.9 48.1 %fusion.1 = f32[96,256]{1,0:T(8,128)S(1)} fusion(f32[1440,256]{1,0:T(8,128)S(1)} %fusion.40), kind=kCustom, calls=%all-reduce-scatter.1 | all-reduce-scatter fusion | flops 393217 | bytes 1573888
  292.0 1.9 collective-permute-start.1
  295.2 2.7 collective-permute-done.1
  298.9 66.9 %all-gather.15.cloned.1.call-done = f32[16,90,256]{2,1,0:T(8,128)} async-done(((f32[1,90,256]{2,1,0:T(8,128)}), f32[16,90,256]{2,1,0:T(8,128)}) %all-gather.15.cloned.1.call-update) | async-done | bytes 1474576 | tf_op jit(solution)/shard_map/all_gather | solution.py:46
  365.9 1.5 reshape.65
  367.4 17.9 %fusion.39 = f32[1440,256]{1,0:T(8,128)S(1)} fusion(f32[1440,256]{1,0:T(8,128)S(1)} %reshape.65, f32[1440,1440]{1,0:T(8,128)} %param.5, f32[]{:T(128)} %bitcast.1, s32[1440]{0:T(1024)S(1)} %get-tuple-element.45, s32[1440]{0:T(1024)S(1)} %get-tuple-element.46), kind=kOutput, calls=%fused_computation.69 | convolution fusion | flops 6376320000 | bytes 11255044 | tf_op jit(solution)/shard_map/dot_general | solution.py:32
  385.2 55.2 %fusion.2 = f32[96,256]{1,0:T(8,128)S(1)} fusion(f32[1440,256]{1,0:T(8,128)S(1)} %fusion.39), kind=kCustom, calls=%all-reduce-scatter.2 | all-reduce-scatter fusion | flops 393217 | bytes 1573888
  440.4 1.3 collective-permute-start.2
  441.7 2.2 collective-permute-done.2
  444.9 10.4 all-gather.19.cloned.1.call-start
  455.3 70.4 %all-gather.17.cloned.1.call-done = f32[16,90,256]{2,1,0:T(8,128)} async-done(((f32[1,90,256]{2,1,0:T(8,128)}), f32[16,90,256]{2,1,0:T(8,128)}) %all-gather.17.cloned.1.call-update) | async-done | bytes 1474576 | tf_op jit(solution)/shard_map/all_gather | solution.py:49
  525.7 1.5 reshape.67
  527.1 10.1 fusion.38
  537.2 48.0 %fusion.3 = f32[96,256]{1,0:T(8,128)S(1)} fusion(f32[1440,256]{1,0:T(8,128)S(1)} %fusion.38), kind=kCustom, calls=%all-reduce-scatter.3 | all-reduce-scatter fusion | flops 393217 | bytes 1573888
  585.2 1.9 collective-permute-start.3
  587.2 4.0 collective-permute-done.3
  591.4 0.7 fusion.16
  592.2 66.9 %all-gather.19.cloned.1.call-done = f32[16,90,256]{2,1,0:T(8,128)} async-done(((f32[1,90,256]{2,1,0:T(8,128)}), f32[16,90,256]{2,1,0:T(8,128)}) %all-gather.19.cloned.1.call-update) | async-done | bytes 1474576 | tf_op jit(solution)/shard_map/all_gather | solution.py:46
  659.1 1.5 reshape.69
  660.6 19.0 %fusion.37 = f32[1440,256]{1,0:T(8,128)} fusion(f32[1440,256]{1,0:T(8,128)S(1)} %reshape.69, f32[1440,1440]{1,0:T(8,128)} %param.5, f32[]{:T(128)} %bitcast.1, s32[1440]{0:T(1024)S(1)} %get-tuple-element.45, s32[1440]{0:T(1024)S(1)} %get-tuple-element.46), kind=kOutput, calls=%fused_computation.67 | convolution fusion | flops 6376320000 | bytes 11255044 | tf_op jit(solution)/shard_map/dot_general | solution.py:32
  679.7 0.8 fusion.8
  680.5 74.2 %fusion.42 = (f32[96,256]{1,0:T(8,128)S(1)}, f32[96,256]{1,0:T(8,128)S(1)}) fusion(f32[1440,256]{1,0:T(8,128)} %fusion.37, f32[1440,256]{1,0:T(8,128)S(1)} %fusion.8), kind=kCustom, calls=%all-reduce-scatter.6 | all-reduce-scatter fusion | flops 786433 | bytes 3146752
  754.7 1.3 collective-permute-start.4
  756.0 1.5 collective-permute-start.5
  758.4 1.1 fusion.21
  759.8 1.1 fusion.14
  761.0 256.2 %all-reduce.17.cloned.1.call-done = (f32[256,256]{0,1:T(8,128)}, f32[256,256]{0,1:T(8,128)}) async-done(((f32[256,256]{0,1:T(8,128)}, f32[256,256]{0,1:T(8,128)}), (f32[256,256]{0,1:T(8,128)}, f32[256,256]{0,1:T(8,128)})) %all-reduce.17.cloned.1.call-update) | async-done | bytes 524304 | tf_op jit(solution)/shard_map/psum | solution.py:86
  1017.2 1.1 copy.16
  1018.3 1.1 bitcast_add_fusion.1
  1019.6 11.7 %cholesky.50 = f32[128,128]{1,0:T(8,128)S(1)} custom-call(f32[128,128]{1,0:T(8,128)S(1)} %cholesky.118), custom_call_target="Cholesky" | custom-call | tf_op jit(solution)/shard_map/jit(cholesky)/cholesky | solution.py:89
  1031.4 9.8 custom-call.14
  1041.7 11.7 %cholesky.105 = f32[128,128]{1,0:T(8,128)S(1)} custom-call(f32[128,128]{1,0:T(8,128)S(1)} %convolution_subtract_fusion.2), custom_call_target="Cholesky" | custom-call | tf_op jit(solution)/shard_map/jit(cholesky)/cholesky | solution.py:89
  1053.4 0.7 compare_reduce_fusion
  1056.2 4.1 while.4
  1056.8 1.4 bitcast_dynamic-update-slice_fusion.2
  1058.8 1.4 bitcast_dynamic-update-slice_fusion.2
  1060.3 19.9 %custom-call.17 = f32[2,128,128]{1,2,0:T(8,128)S(1)} custom-call(f32[2,128,128]{2,1,0:T(8,128)S(1)} %get-tuple-element.18), custom_call_target="InvertDiagBlocksLowerTriangular" | custom-call | tf_op jit(solution)/shard_map/jit(_solve_triangular)/triangular_solve | solution.py:91
  1082.3 0.7 pad_maximum_fusion
  (65 shorter events, 10.8 us)
Async XLA Ops:
  7.2 65.3 %all-gather.11.cloned.1.call-start = ((), (), s32[]{:S(2)}) async-start(), calls=%async_computation | async-start | bytes 1671168 | tf_op jit(solution)/shard_map/all_gather | solution.py:46
  7.9 224.4 %all-gather.13.cloned.1.call-start = ((), (), s32[]{:S(2)}) async-start(), calls=%async_computation.1 | async-start | bytes 1671168 | tf_op jit(solution)/shard_map/all_gather | solution.py:49
  91.8 57.9 %copy-start.2 = (u32[256]{0:T(256)S(1)}, u32[256]{0:T(256)}, u32[]{:S(2)}) copy-start(u32[256]{0:T(256)} %constant.130) | copy-start | bytes 3076
  147.1 3.9 collective-permute-start
  151.9 213.9 %all-gather.15.cloned.1.call-start = ((), (), s32[]{:S(2)}) async-start(), calls=%async_computation.2 | async-start | bytes 1671168 | tf_op jit(solution)/shard_map/all_gather | solution.py:46
  243.8 50.1 %copy-start.1 = (u32[256]{0:T(256)S(1)}, u32[256]{0:T(256)}, u32[]{:S(2)}) copy-start(u32[256]{0:T(256)} %constant.134) | copy-start | bytes 3076
  243.9 54.3 %copy-start = (f32[90,256]{1,0:T(8,128)S(1)}, f32[90,256]{1,0:T(8,128)}, u32[]{:S(2)}) copy-start(f32[90,256]{1,0:T(8,128)} %param.6) | copy-start | bytes 276484
  292.0 5.9 collective-permute-start.1
  298.9 226.8 %all-gather.17.cloned.1.call-start = ((), (), s32[]{:S(2)}) async-start(), calls=%async_computation.3 | async-start | bytes 1671168 | tf_op jit(solution)/shard_map/all_gather | solution.py:49
  440.4 3.5 collective-permute-start.2
  444.9 214.2 %all-gather.19.cloned.1.call-start = ((), (), s32[]{:S(2)}) async-start(), calls=%async_computation.4 | async-start | bytes 1671168 | tf_op jit(solution)/shard_map/all_gather | solution.py:46
  585.2 5.9 collective-permute-start.3
  592.1 425.1 %all-reduce.17.cloned.1.call-start = ((), (), s32[]{:S(2)}) async-start(), calls=%async_computation.5 | async-start | bytes 1048576 | tf_op jit(solution)/shard_map/psum | solution.py:86
  754.7 3.5 collective-permute-start.4
  756.0 3.6 collective-permute-start.5
Sparse Core Ops, SparseCore 0:
  10.7 61.7 all-gather.10
  152.1 80.1 all-gather.12
  299.0 66.7 all-gather.14
  445.0 80.5 all-gather.16
  592.3 66.7 all-gather.18
  761.1 256.0 all-reduce.16
where the time goes:
time: 1100 us; the launch traced here: 1090 us
  waiting for transfers between devices  613 us (56%)
  blocking collectives  281 us (26%)
  matrix products  79.5 us (7%)
  other arithmetic  60 us (5%)
  between operations  20.4 us (2%)
  starting transfers between devices  20.1 us (2%)
  local copies, waits for them, and re-layouts  17.1 us (2%)
    unnamed x5, blocking collectives  281 us
    psum x1, waiting for transfers between devices, body(): gram, projected = lax.psum((gram_part, image_part), ('row', 'col'))  256 us
    all_gather x3, waiting for transfers between devices, gather_rows(): return lax.all_gather(values, 'col', axis=0, tiled=True)  196 us
    all_gather x2, waiting for transfers between devices, gather_cols(): return lax.all_gather(values, 'row', axis=0, tiled=True)  150 us
    dot_general x3, matrix products, through_columns(): lax.dot_general(shifted, panel_rows, (((0,), (0,)), ((), ())), precision=...  54.7 us
    another operation x7, other arithmetic, body(): factor = jnp.linalg.cholesky(gram)  34.6 us
  transfers between devices with their start and end apart: 12, of which 10 were waited for; matrix products, arithmetic and copies ran while one was open for 0% of the time, Pallas kernels for 0%

commit v1 on v0

--- a/solution.py
+++ b/solution.py
@@ -83,7 +83,7 @@
         precision=lax.Precision.HIGHEST,
         preferred_element_type=jnp.float32,
     )
-    gram, projected = lax.psum((gram_part, image_part), ("row", "col"))
+    gram, projected = lax.psum(lax.psum((gram_part, image_part), "col"), "row")
     projected = projected + center * gram
     projected = (projected + projected.T) * 0.5
     factor = jnp.linalg.cholesky(gram)

time: 1100 us -> 1190 us (1.082)
  waiting for transfers between devices: 613 us -> 701 us
    psum x1 -> x2, waiting for transfers between devices: 256 us -> 345 us  [body(): gram, projected = lax.psum(lax.psum((gram_part, image_part), 'col'), 'row')]
  transfers between devices with their start and end apart: 12 -> 13, of which waited for: 10 -> 11; matrix products, arithmetic and copies ran while one was open for 0% -> 0% of each run, Pallas kernels for 0% -> 0%
where the time goes in v1:
time: 1190 us; the launch traced here: 1180 us
  waiting for transfers between devices  701 us (59%)
  blocking collectives  281 us (24%)
  matrix products  79.5 us (7%)
  other arithmetic  59.7 us (5%)
  starting transfers between devices  20.7 us (2%)
  between operations  20.3 us (2%)
  local copies, waits for them, and re-layouts  17 us (1%)
    psum x2, waiting for transfers between devices, body(): gram, projected = lax.psum(lax.psum((gram_part, image_part), 'col'), 'row')  345 us
    unnamed x5, blocking collectives  281 us
    all_gather x3, waiting for transfers between devices, gather_rows(): return lax.all_gather(values, 'col', axis=0, tiled=True)  196 us
    all_gather x2, waiting for transfers between devices, gather_cols(): return lax.all_gather(values, 'row', axis=0, tiled=True)  150 us
    dot_general x3, matrix products, through_columns(): lax.dot_general(shifted, panel_rows, (((0,), (0,)), ((), ())), precision=...  54.7 us
    another operation x7, other arithmetic, body(): factor = jnp.linalg.cholesky(gram)  34.6 us
  transfers between devices with their start and end apart: 13, of which 11 were waited for; matrix products, arithmetic and copies ran while one was open for 0% of the time, Pallas kernels for 0%

profile of v1, /device:TPU:2, one launch (start us, length us, event | category | flops | bytes accessed | tf_op | source)
XLA Modules:
  0.0 1179.3 jit_solution(10831064368036775651)
XLA Ops:
  8.0 1.3 fusion.44
  10.6 61.9 %all-gather.11.cloned.1.call-done = f32[16,90,256]{2,1,0:T(8,128)} async-done(((f32[1,90,256]{2,1,0:T(8,128)}), f32[16,90,256]{2,1,0:T(8,128)}) %all-gather.11.cloned.1.call-update) | async-done | bytes 1474576 | tf_op jit(solution)/shard_map/all_gather | solution.py:46
  72.5 1.5 reshape.61
  74.0 17.9 %fusion.41 = f32[1440,256]{1,0:T(8,128)S(1)} fusion(f32[1440,256]{1,0:T(8,128)S(1)} %reshape.61, f32[1440,1440]{1,0:T(8,128)} %param.5, f32[]{:T(128)} %bitcast.1, s32[1440]{0:T(1024)S(1)} %get-tuple-element.47, s32[1440]{0:T(1024)S(1)} %get-tuple-element.48), kind=kOutput, calls=%fused_computation.71 | convolution fusion | flops 6376320000 | bytes 11255044 | tf_op jit(solution)/shard_map/dot_general | solution.py:32
  91.8 55.3 %fusion = f32[96,256]{1,0:T(8,128)S(1)} fusion(f32[1440,256]{1,0:T(8,128)S(1)} %fusion.41), kind=kCustom, calls=%all-reduce-scatter | all-reduce-scatter fusion | flops 393217 | bytes 1573888
  147.1 1.3 collective-permute-start
  152.2 80.0 %all-gather.13.cloned.1.call-done = f32[16,90,256]{2,1,0:T(8,128)} async-done(((f32[1,90,256]{2,1,0:T(8,128)}), f32[16,90,256]{2,1,0:T(8,128)}) %all-gather.13.cloned.1.call-update) | async-done | bytes 1474576 | tf_op jit(solution)/shard_map/all_gather | solution.py:49
  232.3 1.5 reshape.63
  233.8 10.1 fusion.40
  243.9 48.1 %fusion.1 = f32[96,256]{1,0:T(8,128)S(1)} fusion(f32[1440,256]{1,0:T(8,128)S(1)} %fusion.40), kind=kCustom, calls=%all-reduce-scatter.1 | all-reduce-scatter fusion | flops 393217 | bytes 1573888
  292.0 1.9 collective-permute-start.1
  295.2 2.7 collective-permute-done.1
  298.9 66.9 %all-gather.15.cloned.1.call-done = f32[16,90,256]{2,1,0:T(8,128)} async-done(((f32[1,90,256]{2,1,0:T(8,128)}), f32[16,90,256]{2,1,0:T(8,128)}) %all-gather.15.cloned.1.call-update) | async-done | bytes 1474576 | tf_op jit(solution)/shard_map/all_gather | solution.py:46
  365.9 1.5 reshape.65
  367.4 17.9 %fusion.39 = f32[1440,256]{1,0:T(8,128)S(1)} fusion(f32[1440,256]{1,0:T(8,128)S(1)} %reshape.65, f32[1440,1440]{1,0:T(8,128)} %param.5, f32[]{:T(128)} %bitcast.1, s32[1440]{0:T(1024)S(1)} %get-tuple-element.47, s32[1440]{0:T(1024)S(1)} %get-tuple-element.48), kind=kOutput, calls=%fused_computation.69 | convolution fusion | flops 6376320000 | bytes 11255044 | tf_op jit(solution)/shard_map/dot_general | solution.py:32
  385.2 55.2 %fusion.2 = f32[96,256]{1,0:T(8,128)S(1)} fusion(f32[1440,256]{1,0:T(8,128)S(1)} %fusion.39), kind=kCustom, calls=%all-reduce-scatter.2 | all-reduce-scatter fusion | flops 393217 | bytes 1573888
  440.4 1.3 collective-permute-start.2
  441.7 2.2 collective-permute-done.2
  444.9 11.0 all-gather.19.cloned.1.call-start
  455.9 69.8 %all-gather.17.cloned.1.call-done = f32[16,90,256]{2,1,0:T(8,128)} async-done(((f32[1,90,256]{2,1,0:T(8,128)}), f32[16,90,256]{2,1,0:T(8,128)}) %all-gather.17.cloned.1.call-update) | async-done | bytes 1474576 | tf_op jit(solution)/shard_map/all_gather | solution.py:49
  525.7 1.5 reshape.67
  527.1 10.1 fusion.38
  537.2 47.9 %fusion.3 = f32[96,256]{1,0:T(8,128)S(1)} fusion(f32[1440,256]{1,0:T(8,128)S(1)} %fusion.38), kind=kCustom, calls=%all-reduce-scatter.3 | all-reduce-scatter fusion | flops 393217 | bytes 1573888
  585.2 1.9 collective-permute-start.3
  587.1 4.0 collective-permute-done.3
  591.4 0.7 fusion.16
  592.2 66.8 %all-gather.19.cloned.1.call-done = f32[16,90,256]{2,1,0:T(8,128)} async-done(((f32[1,90,256]{2,1,0:T(8,128)}), f32[16,90,256]{2,1,0:T(8,128)}) %all-gather.19.cloned.1.call-update) | async-done | bytes 1474576 | tf_op jit(solution)/shard_map/all_gather | solution.py:46
  659.0 1.5 reshape.69
  660.5 19.0 %fusion.37 = f32[1440,256]{1,0:T(8,128)} fusion(f32[1440,256]{1,0:T(8,128)S(1)} %reshape.69, f32[1440,1440]{1,0:T(8,128)} %param.5, f32[]{:T(128)} %bitcast.1, s32[1440]{0:T(1024)S(1)} %get-tuple-element.47, s32[1440]{0:T(1024)S(1)} %get-tuple-element.48), kind=kOutput, calls=%fused_computation.67 | convolution fusion | flops 6376320000 | bytes 11255044 | tf_op jit(solution)/shard_map/dot_general | solution.py:32
  679.6 0.8 fusion.8
  680.4 74.2 %fusion.42 = (f32[96,256]{1,0:T(8,128)S(1)}, f32[96,256]{1,0:T(8,128)S(1)}) fusion(f32[1440,256]{1,0:T(8,128)} %fusion.37, f32[1440,256]{1,0:T(8,128)S(1)} %fusion.8), kind=kCustom, calls=%all-reduce-scatter.6 | all-reduce-scatter fusion | flops 786433 | bytes 3146752
  754.6 1.3 collective-permute-start.4
  755.9 1.3 collective-permute-start.5
  757.2 0.9 collective-permute-done.4
  758.4 1.1 fusion.21
  759.7 1.1 fusion.14
  761.2 171.4 %all-reduce.19.cloned.1.call-done = (f32[256,256]{0,1:T(8,128)}, f32[256,256]{0,1:T(8,128)}) async-done(((f32[256,256]{0,1:T(8,128)}, f32[256,256]{0,1:T(8,128)}), (f32[256,256]{0,1:T(8,128)}, f32[256,256]{0,1:T(8,128)})) %all-reduce.19.cloned.1.call-update) | async-done | bytes 524304 | tf_op jit(solution)/shard_map/psum | solution.py:86
  932.6 173.8 %all-reduce.21.cloned.1.call-done = (f32[256,256]{0,1:T(8,128)}, f32[256,256]{0,1:T(8,128)}) async-done(((f32[256,256]{0,1:T(8,128)}, f32[256,256]{0,1:T(8,128)}), (f32[256,256]{0,1:T(8,128)}, f32[256,256]{0,1:T(8,128)})) %all-reduce.21.cloned.1.call-update) | async-done | bytes 524304 | tf_op jit(solution)/shard_map/psum | solution.py:86
  1106.4 1.1 copy.16
  1107.4 1.1 bitcast_add_fusion.1
  1108.7 11.7 cholesky.50
  1120.5 9.8 custom-call.14
  1130.8 11.7 cholesky.105
  1145.2 4.2 while.4
  1146.1 1.4 bitcast_dynamic-update-slice_fusion.2
  1148.0 1.4 bitcast_dynamic-update-slice_fusion.2
  1149.4 19.7 %custom-call.17 = f32[2,128,128]{1,2,0:T(8,128)S(1)} custom-call(f32[2,128,128]{2,1,0:T(8,128)S(1)} %get-tuple-element.18), custom_call_target="InvertDiagBlocksLowerTriangular" | custom-call | tf_op jit(solution)/shard_map/jit(_solve_triangular)/triangular_solve | solution.py:91
  1171.3 0.7 pad_maximum_fusion
  (68 shorter events, 11.8 us)
Async XLA Ops:
  7.2 65.3 %all-gather.11.cloned.1.call-start = ((), (), s32[]{:S(2)}) async-start(), calls=%async_computation | async-start | bytes 1671168 | tf_op jit(solution)/shard_map/all_gather | solution.py:46
  7.9 224.4 %all-gather.13.cloned.1.call-start = ((), (), s32[]{:S(2)}) async-start(), calls=%async_computation.1 | async-start | bytes 1671168 | tf_op jit(solution)/shard_map/all_gather | solution.py:49
  91.8 57.9 %copy-start.2 = (u32[256]{0:T(256)S(1)}, u32[256]{0:T(256)}, u32[]{:S(2)}) copy-start(u32[256]{0:T(256)} %constant.130) | copy-start | bytes 3076
  147.1 3.9 collective-permute-start
  151.9 213.9 %all-gather.15.cloned.1.call-start = ((), (), s32[]{:S(2)}) async-start(), calls=%async_computation.2 | async-start | bytes 1671168 | tf_op jit(solution)/shard_map/all_gather | solution.py:46
  243.8 50.1 %copy-start.1 = (u32[256]{0:T(256)S(1)}, u32[256]{0:T(256)}, u32[]{:S(2)}) copy-start(u32[256]{0:T(256)} %constant.134) | copy-start | bytes 3076
  243.9 54.3 %copy-start = (f32[90,256]{1,0:T(8,128)S(1)}, f32[90,256]{1,0:T(8,128)}, u32[]{:S(2)}) copy-start(f32[90,256]{1,0:T(8,128)} %param.6) | copy-start | bytes 276484
  292.0 5.9 collective-permute-start.1
  298.9 226.8 %all-gather.17.cloned.1.call-start = ((), (), s32[]{:S(2)}) async-start(), calls=%async_computation.3 | async-start | bytes 1671168 | tf_op jit(solution)/shard_map/all_gather | solution.py:49
  440.4 3.5 collective-permute-start.2
  444.9 214.1 %all-gather.19.cloned.1.call-start = ((), (), s32[]{:S(2)}) async-start(), calls=%async_computation.4 | async-start | bytes 1671168 | tf_op jit(solution)/shard_map/all_gather | solution.py:46
  585.2 5.9 collective-permute-start.3
  592.1 340.4 %all-reduce.19.cloned.1.call-start = ((), (), s32[]{:S(2)}) async-start(), calls=%async_computation.5 | async-start | bytes 1048576 | tf_op jit(solution)/shard_map/psum | solution.py:86
  754.6 3.5 collective-permute-start.4
  755.9 3.6 collective-permute-start.5
  760.9 345.5 %all-reduce.21.cloned.1.call-start = ((), (), s32[]{:S(2)}) async-start(), calls=%async_computation.6 | async-start | bytes 1048576 | tf_op jit(solution)/shard_map/psum | solution.py:86
Sparse Core Ops, SparseCore 0:
  10.7 61.7 all-gather.10
  152.1 80.1 all-gather.12
  299.0 66.7 all-gather.14
  445.0 80.5 all-gather.16
  592.2 66.7 all-gather.18
  761.0 171.4 all-reduce.18
  935.2 171.1 all-reduce.20
